TPU v7x, 32 devices: a whole 2x2x4 slice. The times are simulated.
32 devices in a mesh: amp: 4 (over y, core), own: 8 (over z, x).
Axes of the slice: x: 2, y: 2, z: 4, core: 2. Of those that a mesh axis runs over, the one named last changes fastest.
Arguments:
- amplitudes: bfloat16 [32, 2304, 192], P('own', None, 'amp'), may hold values from -6 to 6
- integrals: bfloat16 [32, 1152, 2304], P('own'), as said below
- occ_irrep: int32 [34], replicated, may hold values from 0 to 7, as said below
- tile_irrep: int32 [18], replicated, may hold values from 0 to 7, as said below
Outputs:
- cycle_term: bfloat16 [2304, 2304], P(('amp', 'own'))
Inputs may be any that keep to these rules, and one draw needn't show every extreme that they name: `occ_irrep`: labels of the D2h group, combined by XOR; every label occurs, and all labels occur equally often up to one. `tile_irrep`: labels of the D2h group, combined by XOR; every label occurs, and all labels occur equally often up to one, so some label has exactly 3 tiles. integrals[k, c, (j, b)] is zero unless the labels of k, c, j and b combine by XOR to 0.
All inputs are finite; a program needn't handle non-finite values.
Results may differ from a plain program's by a relative error of at most 0.001.
Values may be sent and summed in bfloat16 or wider, within the bound.
A program may use at most 128 MiB of HBM per device.

v0:
```python
import jax
import jax.numpy as jnp
from jax import lax
from jax.sharding import PartitionSpec as P

V = 1152
TILE = 64
NI = 2


def tile_ranks(tile_irrep):
    count = tile_irrep.shape[0]
    index = jnp.arange(count, dtype=jnp.int32)
    same = (tile_irrep[:, None] == tile_irrep[None, :]) & (index[None, :] < index[:, None])
    return jnp.sum(same.astype(jnp.int32), axis=1)


def shards(amplitudes, integrals, occ_irrep, tile_irrep):
    amp_index = lax.axis_index("amp")
    own_index = lax.axis_index("own")
    n_amp = lax.axis_size("amp")
    n_own = lax.axis_size("own")
    regrouped = lax.all_to_all(amplitudes, "amp", split_axis=1, concat_axis=2, tiled=True)
    k_local, rows, packed_width = regrouped.shape
    slot_count = packed_width // TILE
    virt_lab = jnp.repeat(tile_irrep, TILE)
    row_all = jnp.bitwise_xor(jnp.repeat(occ_irrep[:NI], V), jnp.tile(virt_lab, NI))
    row_lab = lax.dynamic_slice_in_dim(row_all, amp_index * rows, rows)
    k_lab = lax.dynamic_slice_in_dim(occ_irrep, NI + own_index * k_local, k_local)
    wanted = jnp.bitwise_xor(k_lab[:, None], row_lab[None, :])
    ranks = tile_ranks(tile_irrep)
    slot_ids = jnp.arange(slot_count, dtype=jnp.int32)
    select = (tile_irrep[None, None, None, :] == wanted[:, :, None, None]) & (
        ranks[None, None, None, :] == slot_ids[None, None, :, None]
    )
    pieces = regrouped.reshape(k_local, rows, slot_count, TILE)
    dense = jnp.einsum(
        "krjt,krje->krte", select.astype(jnp.bfloat16), pieces, preferred_element_type=jnp.float32
    )
    masked = dense.reshape(k_local, rows, V).astype(jnp.bfloat16)
    summed = lax.psum_scatter(
        jnp.einsum("kmc,kcn->mn", masked, integrals, preferred_element_type=jnp.float32),
        "own",
        scatter_dimension=0,
        tiled=True,
    )
    share = summed.shape[0]
    blocks = summed.reshape(share, n_amp, n_own, share)
    moved = lax.all_to_all(
        lax.all_to_all(blocks, "amp", split_axis=1, concat_axis=1, tiled=True),
        "own",
        split_axis=2,
        concat_axis=2,
        tiled=True,
    )
    mirrored = jnp.transpose(moved, (3, 1, 2, 0)).reshape(share, NI * V)
    return (summed + mirrored).astype(jnp.bfloat16)


def solution(mesh):
    return jax.shard_map(
        shards,
        mesh=mesh,
        in_specs=(P("own", None, "amp"), P("own", None, None), P(), P()),
        out_specs=P(("amp", "own"), None),
        check_vma=False,
    )
```

profile of v0, /device:TPU:0, one launch (start us, length us, event | category | flops | bytes accessed | tf_op | source)
XLA Modules:
  0.0 252.3 jit_solution(9332235532349839505)
XLA Ops:
  6.5 3.6 %copy.25 = bf16[4,2304,48]{2,0,1:T(4,128)(2,1)S(1)} copy(bf16[4,2304,48]{1,2,0:T(8,128)(2,1)} %param.4) | data formatting | bytes 1769472 | tf_op args[0]
  10.1 0.0 copy-start.1
  10.1 0.0 copy-start.2
  10.1 4.6 %reshape.80 = bf16[4,2,55296]{2,1,0:T(2,128)(2,1)} reshape(bf16[2304,4,48]{2,1,0:T(4,128)(2,1)S(1)} %bitcast.18) | data formatting | bytes 1769472
  14.8 4.2 %all-to-all-start = ((bf16[4,2,55296]{2,1,0:T(2,128)(2,1)}), bf16[4,2,55296]{2,1,0:T(2,128)(2,1)S(1)}, u32[]{:S(2)}, u32[]{:S(2)}) async-start(bf16[4,2,55296]{2,1,0:T(2,128)(2,1)} %reshape.80), calls=%async_computation | async-start | bytes 1769472 | tf_op jit(solution)/shard_map/all_to_all | solution.py:23
  19.0 0.0 reduce-scatter.2.cloned.1.call-start
  19.0 0.0 copy-done.1
  19.0 0.2 convert_reduce_fusion
  19.2 0.1 broadcast_in_dim.5
  19.3 0.1 tile.8
  19.3 0.0 copy-done.2
  19.3 0.1 dynamic_slice.6
  19.4 0.1 broadcast_xor_fusion.1
  19.5 0.1 dynamic_slice.7
  19.6 0.1 broadcast_xor_fusion
  19.7 1.1 broadcast_compare_fusion
  20.8 10.9 %all-to-all-done = bf16[4,2,55296]{2,1,0:T(2,128)(2,1)S(1)} async-done(((bf16[4,2,55296]{2,1,0:T(2,128)(2,1)}), bf16[4,2,55296]{2,1,0:T(2,128)(2,1)S(1)}, u32[]{:S(2)}, u32[]{:S(2)}) %all-to-all-start) | async-done | bytes 884768 | tf_op jit(solution)/shard_map/all_to_all | solution.py:23
  31.7 2.4 reshape.81
  34.1 1.5 copy.27
  35.6 1.5 copy.28
  37.1 11.1 %convolution_convert_fusion = bf16[4,576,18,64]{3,2,1,0:T(8,128)(2,1)} fusion(bf16[4,576,3,64]{3,2,1,0:T(4,128)(2,1)S(1)} %copy.28, pred[3,18]{1,0:T(4,128)(4,1)S(1)} %iota_compare_fusion.1, pred[4,576,18]{2,1,0:T(8,128)(4,1)} %broadcast_compare_fusion), kind=kOutput, calls=%fused_computation | convolution fusion | flops 18703872 | bytes 6234678 | tf_op jit(solution)/shard_map/krjt,krje->krte/dot_general | solution.py:37
  48.2 15.5 %copy.29 = bf16[4,576,18,64]{1,3,2,0:T(8,128)(2,1)} copy(bf16[4,576,18,64]{3,2,1,0:T(8,128)(2,1)} %convolution_convert_fusion) | data formatting | bytes 10616832 | tf_op jit(solution)/shard_map/convert_element_type | solution.py:40
  63.7 19.2 %convolution_bitcast_fusion = f32[576,2304]{1,0:T(8,128)} fusion(bf16[4,576,1152]{1,2,0:T(8,128)(2,1)} %bitcast.19, bf16[4,1152,2304]{2,1,0:T(8,128)(2,1)} %param.5), kind=kOutput, calls=%fused_computation.1 | convolution fusion | flops 12230590464 | bytes 31850496 | tf_op jit(solution)/shard_map/kmc,kcn->mn/dot_general | solution.py:42
  82.8 0.0 reduce-scatter.2.cloned.1.call-update
  82.9 105.3 %reduce-scatter.2.cloned.1.call-done = f32[72,2304]{1,0:T(8,128)} async-done(((f32[576,2304]{1,0:T(8,128)}), f32[72,2304]{1,0:T(8,128)}) %reduce-scatter.2.cloned.1.call-update) | async-done | bytes 663568 | tf_op jit(solution)/shard_map/reduce_scatter | solution.py:41
  188.2 2.3 reshape.77
  190.5 0.9 copy.31
  191.4 18.4 %all_to_all.25 = f32[72,4,8,72]{0,2,3,1:T(8,128)S(1)} all-to-all(f32[72,4,8,72]{0,2,3,1:T(8,128)S(1)} %copy.31), channel_id=1, replica_groups=mesh['amp'=4,'own'=8] {'amp'}, dimensions={1} | all-to-all | bytes 1327104 | tf_op jit(solution)/shard_map/all_to_all | solution.py:50
  209.8 0.8 copy.32
  210.6 32.7 %all_to_all.26 = f32[72,4,8,72]{0,1,3,2:T(4,128)S(1)} all-to-all(f32[72,4,8,72]{0,1,3,2:T(4,128)S(1)} %copy.32), channel_id=1, replica_groups=mesh['amp'=4,'own'=8] {'own'}, dimensions={2} | all-to-all | bytes 1327104 | tf_op jit(solution)/shard_map/all_to_all | solution.py:49
  243.3 0.0 copy-start
  243.3 0.7 copy.33
  244.0 0.6 reshape.78
  244.7 0.0 copy-done
  244.7 0.8 add_convert_fusion
  (2 shorter events, 0.0 us)
Async XLA Ops:
  10.1 8.9 %copy-start.1 = (s32[18]{0:T(128)S(1)}, s32[18]{0:T(128)}, u32[]{:S(2)}) copy-start(s32[18]{0:T(128)} %param.7) | copy-start | bytes 220
  10.1 9.2 %copy-start.2 = (s32[34]{0:T(128)S(1)}, s32[34]{0:T(128)}, u32[]{:S(2)}) copy-start(s32[34]{0:T(128)} %param.6) | copy-start | bytes 412
  14.8 16.9 %all-to-all-start = ((bf16[4,2,55296]{2,1,0:T(2,128)(2,1)}), bf16[4,2,55296]{2,1,0:T(2,128)(2,1)S(1)}, u32[]{:S(2)}, u32[]{:S(2)}) async-start(bf16[4,2,55296]{2,1,0:T(2,128)(2,1)} %reshape.80), calls=%async_computation | async-start | bytes 1769472 | tf_op jit(solution)/shard_map/all_to_all | solution.py:23
  19.0 169.2 %reduce-scatter.2.cloned.1.call-start = ((), (), s32[]{:S(2)}) async-start(), calls=%async_computation.4 | async-start | bytes 5971968 | tf_op jit(solution)/shard_map/reduce_scatter | solution.py:41
  243.3 1.3 copy-start
Sparse Core Ops, SparseCore 0:
  83.0 105.1 reduce-scatter.1
where the time goes:
time: 253 us; the launch traced here: 252 us
  waiting for transfers between devices  116 us (46%)
  blocking collectives  51.1 us (20%)
  local copies, waits for them, and re-layouts  34.7 us (14%)
  matrix products  30.3 us (12%)
  between operations  13.5 us (5%)
  starting transfers between devices  4.24 us (2%)
    reduce_scatter x1, waiting for transfers between devices, shards(): lax.psum_scatter(jnp.einsum('kmc,kcn->mn', masked, integrals, preferred_e...  105 us
    all_to_all x1, blocking collectives, shards(): lax.all_to_all(lax.all_to_all(blocks, 'amp', split_axis=1, concat_axis=1,...  32.7 us
    dot_general x1, matrix products, shards(): jnp.einsum('kmc,kcn->mn', masked, integrals, preferred_element_type=jnp.f...  19.2 us
    all_to_all x1, blocking collectives, shards(): lax.all_to_all(blocks, 'amp', split_axis=1, concat_axis=1, tiled=True)  18.4 us
    convert_element_type x1, local copies, waits for them, and re-layouts, shards(): masked = dense.reshape(k_local, rows, V).astype(jnp.bfloat16)  15.5 us
    dot_general x1, matrix products, shards(): jnp.einsum('krjt,krje->krte', select.astype(jnp.bfloat16), pieces, prefer...  11.1 us
    all_to_all x1, waiting for transfers between devices, shards(): lax.all_to_all(amplitudes, 'amp', split_axis=1, concat_axis=2, tiled=True)  10.9 us
    unnamed x9, local copies, waits for them, and re-layouts  10.6 us
  transfers between devices with their start and end apart: 2, of which 2 were waited for; matrix products, arithmetic and copies ran while one was open for 1% of the time, Pallas kernels for 0%

commit v1 on v0

--- a/solution.py
+++ b/solution.py
@@ -20,7 +20,19 @@
     own_index = lax.axis_index("own")
     n_amp = lax.axis_size("amp")
     n_own = lax.axis_size("own")
-    regrouped = lax.all_to_all(amplitudes, "amp", split_axis=1, concat_axis=2, tiled=True)
+
+    def track_plate_by_axis(local_x):
+        return jnp.concatenate(
+            lax.all_to_all(
+                jnp.stack(jnp.split(local_x, lax.axis_size("amp"), axis=1)),
+                axis_name="amp",
+                split_axis=0,
+                concat_axis=0,
+            ),
+            2,
+        )
+
+    regrouped = track_plate_by_axis(amplitudes)
     k_local, rows, packed_width = regrouped.shape
     slot_count = packed_width // TILE
     virt_lab = jnp.repeat(tile_irrep, TILE)

time: 253 us -> 245 us (0.968)
  local copies, waits for them, and re-layouts: 34.7 us -> 24.1 us
    unnamed x9 -> x6, local copies, waits for them, and re-layouts: 10.6 us -> 0.02 us
    another operation x0 -> x2, local copies, waits for them, and re-layouts: none -> 2.96 us  [the longest x1 1.52 us: shards(): pieces = regrouped.reshape(k_local, rows, slot_count, TILE)]
where the time goes in v1:
time: 245 us; the launch traced here: 244 us
  waiting for transfers between devices  117 us (48%)
  blocking collectives  51.1 us (21%)
  matrix products  30.3 us (12%)
  local copies, waits for them, and re-layouts  24.1 us (10%)
  between operations  13.5 us (6%)
  starting transfers between devices  4.24 us (2%)
  other arithmetic  3.42 us (1%)
    reduce_scatter x1, waiting for transfers between devices, shards(): lax.psum_scatter(jnp.einsum('kmc,kcn->mn', masked, integrals, preferred_e...  105 us
    all_to_all x1, blocking collectives, shards(): lax.all_to_all(lax.all_to_all(blocks, 'amp', split_axis=1, concat_axis=1,...  32.7 us
    dot_general x1, matrix products, shards(): jnp.einsum('kmc,kcn->mn', masked, integrals, preferred_element_type=jnp.f...  19.2 us
    all_to_all x1, blocking collectives, shards(): lax.all_to_all(blocks, 'amp', split_axis=1, concat_axis=1, tiled=True)  18.4 us
    convert_element_type x1, local copies, waits for them, and re-layouts, shards(): masked = dense.reshape(k_local, rows, V).astype(jnp.bfloat16)  15.4 us
    all_to_all x1, waiting for transfers between devices, track_plate_by_axis(): lax.all_to_all(jnp.stack(jnp.split(local_x, lax.axis_size('amp'), axis=1)...  12 us
    dot_general x1, matrix products, shards(): jnp.einsum('krjt,krje->krte', select.astype(jnp.bfloat16), pieces, prefer...  11.1 us
  transfers between devices with their start and end apart: 2, of which 2 were waited for; matrix products, arithmetic and copies ran while one was open for 1% of the time, Pallas kernels for 0%

profile of v1, /device:TPU:0, one launch (start us, length us, event | category | flops | bytes accessed | tf_op | source)
XLA Modules:
  0.0 244.0 jit_solution(822453945313573416)
XLA Ops:
  6.5 1.4 slice_bitcast_fusion.3
  8.0 0.0 copy-start.1
  8.0 0.0 copy-start.2
  8.0 1.2 pad_maximum_fusion
  9.2 4.2 %all-to-all-start = ((bf16[4,4,576,48]{2,3,1,0:T(8,128)(2,1)}), bf16[4,4,576,48]{2,3,1,0:T(8,128)(2,1)S(1)}, u32[]{:S(2)}, u32[]{:S(2)}) async-start(bf16[4,4,576,48]{2,3,1,0:T(8,128)(2,1)} %pad_maximum_fusion), calls=%async_computation | async-start | bytes 1966080 | tf_op jit(solution)/shard_map/all_to_all | solution.py:26
  13.4 0.0 reduce-scatter.2.cloned.1.call-start
  13.4 0.0 copy-done.1
  13.4 0.2 convert_reduce_fusion
  13.6 0.1 broadcast_in_dim.5
  13.7 0.1 tile.8
  13.7 0.0 copy-done.2
  13.7 0.1 dynamic_slice.6
  13.8 0.1 broadcast_xor_fusion.1
  13.9 0.1 dynamic_slice.7
  14.0 0.1 broadcast_xor_fusion
  14.1 1.1 broadcast_compare_fusion
  15.2 12.0 %all-to-all-done = bf16[4,4,576,48]{2,3,1,0:T(8,128)(2,1)S(1)} async-done(((bf16[4,4,576,48]{2,3,1,0:T(8,128)(2,1)}), bf16[4,4,576,48]{2,3,1,0:T(8,128)(2,1)S(1)}, u32[]{:S(2)}, u32[]{:S(2)}) %all-to-all-start) | async-done | bytes 884768 | tf_op jit(solution)/shard_map/all_to_all | solution.py:26
  27.2 0.1 copy.18
  27.3 1.5 copy.19
  28.8 11.1 %convolution_convert_fusion = bf16[4,576,18,64]{3,2,1,0:T(8,128)(2,1)} fusion(bf16[4,576,3,64]{3,2,1,0:T(4,128)(2,1)S(1)} %copy.19, pred[3,18]{1,0:T(4,128)(4,1)S(1)} %iota_compare_fusion.1, pred[4,576,18]{2,1,0:T(8,128)(4,1)} %broadcast_compare_fusion), kind=kOutput, calls=%fused_computation | convolution fusion | flops 18703872 | bytes 6234678 | tf_op jit(solution)/shard_map/krjt,krje->krte/dot_general | solution.py:49
  39.9 15.4 %copy.20 = bf16[4,576,18,64]{1,3,2,0:T(8,128)(2,1)} copy(bf16[4,576,18,64]{3,2,1,0:T(8,128)(2,1)} %convolution_convert_fusion) | data formatting | bytes 10616832 | tf_op jit(solution)/shard_map/convert_element_type | solution.py:52
  55.3 19.2 %convolution_bitcast_fusion = f32[576,2304]{1,0:T(8,128)} fusion(bf16[4,576,1152]{1,2,0:T(8,128)(2,1)} %bitcast.21, bf16[4,1152,2304]{2,1,0:T(8,128)(2,1)} %param.5), kind=kOutput, calls=%fused_computation.1 | convolution fusion | flops 12230590464 | bytes 31850496 | tf_op jit(solution)/shard_map/kmc,kcn->mn/dot_general | solution.py:54
  74.5 0.0 reduce-scatter.2.cloned.1.call-update
  74.5 105.4 %reduce-scatter.2.cloned.1.call-done = f32[72,2304]{1,0:T(8,128)} async-done(((f32[576,2304]{1,0:T(8,128)}), f32[72,2304]{1,0:T(8,128)}) %reduce-scatter.2.cloned.1.call-update) | async-done | bytes 663568 | tf_op jit(solution)/shard_map/reduce_scatter | solution.py:53
  179.8 2.3 reshape.76
  182.2 0.9 copy.22
  183.1 18.4 %all_to_all.15 = f32[72,4,8,72]{0,2,3,1:T(8,128)S(1)} all-to-all(f32[72,4,8,72]{0,2,3,1:T(8,128)S(1)} %copy.22), channel_id=1, replica_groups=mesh['amp'=4,'own'=8] {'amp'}, dimensions={1} | all-to-all | bytes 1327104 | tf_op jit(solution)/shard_map/all_to_all | solution.py:62
  201.5 0.8 copy.23
  202.3 32.7 %all_to_all.16 = f32[72,4,8,72]{0,1,3,2:T(4,128)S(1)} all-to-all(f32[72,4,8,72]{0,1,3,2:T(4,128)S(1)} %copy.23), channel_id=1, replica_groups=mesh['amp'=4,'own'=8] {'own'}, dimensions={2} | all-to-all | bytes 1327104 | tf_op jit(solution)/shard_map/all_to_all | solution.py:61
  235.0 0.0 copy-start
  235.0 0.7 copy.24
  235.7 0.6 reshape.77
  236.3 0.0 copy-done
  236.3 0.8 add_convert_fusion
  (2 shorter events, 0.0 us)
Async XLA Ops:
  8.0 5.4 %copy-start.1 = (s32[18]{0:T(128)S(1)}, s32[18]{0:T(128)}, u32[]{:S(2)}) copy-start(s32[18]{0:T(128)} %param.7) | copy-start | bytes 220
  8.0 5.7 %copy-start.2 = (s32[34]{0:T(128)S(1)}, s32[34]{0:T(128)}, u32[]{:S(2)}) copy-start(s32[34]{0:T(128)} %param.6) | copy-start | bytes 412
  9.2 18.0 %all-to-all-start = ((bf16[4,4,576,48]{2,3,1,0:T(8,128)(2,1)}), bf16[4,4,576,48]{2,3,1,0:T(8,128)(2,1)S(1)}, u32[]{:S(2)}, u32[]{:S(2)}) async-start(bf16[4,4,576,48]{2,3,1,0:T(8,128)(2,1)} %pad_maximum_fusion), calls=%async_computation | async-start | bytes 1966080 | tf_op jit(solution)/shard_map/all_to_all | solution.py:26
  13.4 166.4 %reduce-scatter.2.cloned.1.call-start = ((), (), s32[]{:S(2)}) async-start(), calls=%async_computation.4 | async-start | bytes 5971968 | tf_op jit(solution)/shard_map/reduce_scatter | solution.py:53
  235.0 1.3 copy-start
Sparse Core Ops, SparseCore 0:
  74.6 105.1 reduce-scatter.1
